TPU v7x, 32 devices: a whole 2x2x4 slice. The times are simulated.
32 devices in a mesh: dp: 8 (over z, x), bn: 4 (over y, core).
Axes of the slice: x: 2, y: 2, z: 4, core: 2. Of those that a mesh axis runs over, the one named last changes fastest.
Arguments:
- features: bfloat16 [512, 8, 2048], P(('dp', 'bn')), may hold values from -6 to 6
- shuffle_masks: int32 [16], replicated, may hold values from 0 to 7, as said below
- conv_in: bfloat16 [2048, 512], replicated, may hold values from -0.125 to 0.125
- conv_mid: bfloat16 [3, 512, 512], replicated, may hold values from -0.15625 to 0.15625
- conv_out: bfloat16 [512, 2048], replicated, may hold values from -0.25 to 0.25
- head: bfloat16 [2048, 128], replicated, may hold values from -0.125 to 0.125
- queries: bfloat16 [512, 128], P(('dp', 'bn'))
- queue: bfloat16 [65536, 128], P('dp')
- positive: int32 [512], P(('dp', 'bn')), may hold values from 0 to 511, as said below
Outputs:
- loss_rows: float32 [512], P(('dp', 'bn'))
Inputs may be any that keep to these rules, and one draw needn't show every extreme that they name: `shuffle_masks`: every binary digit of a dp index is set in exactly half of the entries. positive[i] names a crop with the same bn index as crop i.
All inputs are finite; a program needn't handle non-finite values.
Results may differ from a plain program's by a relative error of at most 0.0023.
Values may be sent and summed in bfloat16 or wider, within the bound.
A program may use at most 64 MiB of HBM per device.

v0:
```python
import jax
import jax.numpy as jnp
from jax import lax
from jax.sharding import PartitionSpec as P

EPS_BN = 1e-05
EPS_UNIT = 1e-06
INV_TEMP = 1.0 / 0.07


def partner_2(value, axis, distance):
    return lax.ppermute(value, axis, [(i, i ^ 1 << distance) for i in range(lax.axis_size(axis))])


def unit_rows(values):
    values = values.astype(jnp.float32)
    return values * lax.rsqrt(jnp.sum(values * values, axis=-1, keepdims=True) + EPS_UNIT)


def group_norm(values, row_total):
    first = lax.psum(jnp.sum(values, axis=0), "bn")
    center = first / row_total
    spread = lax.psum(jnp.sum(jnp.square(values - center), axis=0), "bn") / row_total
    return (values - center) * lax.rsqrt(spread + EPS_BN)


def moving_slots(shuffle_masks, level, half):
    flags = jnp.bitwise_and(jnp.right_shift(shuffle_masks, level), 1)
    return jnp.argsort(1 - flags, stable=True)[:half]


def on_device(features, shuffle_masks, conv_in, conv_mid, conv_out, head, queries, queue, positive):
    dp_count = lax.axis_size("dp")
    bn_count = lax.axis_size("bn")
    bit_count = dp_count.bit_length() - 1
    crop_dev, positions, channels = features.shape
    half = crop_dev // 2
    middle = conv_in.shape[1]
    query_unit = unit_rows(queries).astype(jnp.bfloat16)
    query_all = lax.all_gather(query_unit, "dp", axis=0, tiled=True)
    shuffled = features
    for level in range(bit_count):
        moving = moving_slots(shuffle_masks, level, half)
        partner = partner_2(jnp.take(shuffled, moving, axis=0), "dp", level)
        shuffled = shuffled.at[moving].set(partner)
    row_total = crop_dev * positions * bn_count
    flat_rows = shuffled.reshape(crop_dev * positions, channels)
    first_sum = jnp.dot(flat_rows, conv_in, preferred_element_type=jnp.float32)
    first_act = jax.nn.relu(group_norm(first_sum, row_total)).astype(jnp.bfloat16)
    tap_maps = first_act.reshape(crop_dev, positions, middle)
    padded = jnp.pad(tap_maps, ((0, 0), (1, 1), (0, 0)))
    stacked = jnp.concatenate([padded[:, tap : tap + positions, :] for tap in range(3)], axis=2)
    second_sum = jnp.dot(
        stacked.reshape(crop_dev * positions, 3 * middle),
        conv_mid.reshape(3 * middle, middle),
        preferred_element_type=jnp.float32,
    )
    second_act = jax.nn.relu(group_norm(second_sum, row_total)).astype(jnp.bfloat16)
    third_sum = jnp.dot(second_act, conv_out, preferred_element_type=jnp.float32)
    block = jax.nn.relu(group_norm(third_sum, row_total) + flat_rows.astype(jnp.float32)).astype(
        jnp.bfloat16
    )
    pooled = jnp.mean(
        block.reshape(crop_dev, positions, channels).astype(jnp.float32), axis=1
    ).astype(jnp.bfloat16)
    key_unit = unit_rows(jnp.dot(pooled, head, preferred_element_type=jnp.float32)).astype(
        jnp.bfloat16
    )
    for level in range(bit_count):
        moving = moving_slots(shuffle_masks, level, half)
        partner = partner_2(jnp.take(key_unit, moving, axis=0), "dp", level)
        key_unit = key_unit.at[moving].set(partner)
    queue_unit = unit_rows(queue).astype(jnp.bfloat16)
    scores = jnp.dot(query_all, queue_unit.T, preferred_element_type=jnp.float32) * INV_TEMP
    queue_part = jnp.sum(jnp.exp(scores - INV_TEMP), axis=1)
    key_all = lax.all_gather(key_unit, "dp", axis=0, tiled=True)
    slot_of = positive % crop_dev
    column = positive // crop_dev // bn_count
    picked = jnp.take(key_all, column * crop_dev + slot_of, axis=0)
    positive_logit = (
        jnp.sum(query_unit.astype(jnp.float32) * picked.astype(jnp.float32), axis=-1) * INV_TEMP
    )
    negative = lax.psum_scatter(queue_part, "dp", scatter_dimension=0, tiled=True)
    return jnp.log(jnp.exp(positive_logit - INV_TEMP) + negative) + INV_TEMP - positive_logit


def solution(mesh):
    return jax.shard_map(
        on_device,
        mesh=mesh,
        in_specs=(
            P(("dp", "bn"), None, None),
            P(),
            P(),
            P(),
            P(),
            P(),
            P(("dp", "bn"), None),
            P("dp", None),
            P(("dp", "bn")),
        ),
        out_specs=P(("dp", "bn")),
        check_vma=False,
    )
```

profile of v0, /device:TPU:0, one launch (start us, length us, event | category | flops | bytes accessed | tf_op | source)
XLA Modules:
  0.0 185.4 jit_solution(4941348804758811431)
XLA Ops:
  3.8 3.0 %collective-permute-start = (bf16[8,8,2048]{2,1,0:T(8,128)(2,1)S(1)}, bf16[8,8,2048]{2,1,0:T(8,128)(2,1)S(1)}, u32[]{:S(2)}, u32[]{:S(2)}) collective-permute-start(bf16[8,8,2048]{2,1,0:T(8,128)(2,1)S(1)} %broadcast_select_fusion.2), channel_id=1, source_target_pairs={{0,4},{4,0},{8,12},{12,8},{16,20},{20,16},{24,28},{28,24},{1,5},{5... | collective-permute-start | bytes 786440 | tf_op jit(solution)/shard_map/ppermute | solution.py:12
  9.3 3.8 %collective-permute-done = bf16[8,8,2048]{2,1,0:T(8,128)(2,1)S(1)} collective-permute-done((bf16[8,8,2048]{2,1,0:T(8,128)(2,1)S(1)}, bf16[8,8,2048]{2,1,0:T(8,128)(2,1)S(1)}, u32[]{:S(2)}, u32[]{:S(2)}) %collective-permute-start) | collective-permute-done | bytes 262176 | tf_op jit(solution)/shard_map/ppermute | solution.py:12
  14.5 1.9 %collective-permute-start.1 = (bf16[8,8,2048]{2,1,0:T(8,128)(2,1)S(1)}, bf16[8,8,2048]{2,1,0:T(8,128)(2,1)S(1)}, u32[]{:S(2)}, u32[]{:S(2)}) collective-permute-start(bf16[8,8,2048]{2,1,0:T(8,128)(2,1)S(1)} %broadcast_select_fusion.1), channel_id=1, source_target_pairs={{0,8},{4,12},{8,0},{12,4},{16,24},{20,28},{24,16},{28,20},{1,9},{5... | collective-permute-start | bytes 786440 | tf_op jit(solution)/shard_map/ppermute | solution.py:12
  16.4 2.7 %fusion.2 = f32[8192]{0:T(1024)S(1)} fusion(bf16[8192,128]{1,0:T(8,128)(2,1)} %param.20), kind=kLoop, calls=%fused_computation.18 | loop fusion | flops 3137536 | bytes 2129920 | tf_op jit(solution)/shard_map/reduce_sum | solution.py:17
  19.2 2.9 %collective-permute-done.1 = bf16[8,8,2048]{2,1,0:T(8,128)(2,1)S(1)} collective-permute-done((bf16[8,8,2048]{2,1,0:T(8,128)(2,1)S(1)}, bf16[8,8,2048]{2,1,0:T(8,128)(2,1)S(1)}, u32[]{:S(2)}, u32[]{:S(2)}) %collective-permute-start.1) | collective-permute-done | bytes 262176 | tf_op jit(solution)/shard_map/ppermute | solution.py:12
  23.5 2.6 %collective-permute-start.2 = (bf16[8,8,2048]{2,1,0:T(8,128)(2,1)S(1)}, bf16[8,8,2048]{2,1,0:T(8,128)(2,1)S(1)}, u32[]{:S(2)}, u32[]{:S(2)}) collective-permute-start(bf16[8,8,2048]{2,1,0:T(8,128)(2,1)S(1)} %broadcast_select_fusion), channel_id=1, source_target_pairs={{0,16},{4,20},{8,24},{12,28},{16,0},{20,4},{24,8},{28,12},{1,17},{... | collective-permute-start | bytes 786440 | tf_op jit(solution)/shard_map/ppermute | solution.py:12
  26.2 10.5 %collective-permute-done.2 = bf16[8,8,2048]{2,1,0:T(8,128)(2,1)S(1)} collective-permute-done((bf16[8,8,2048]{2,1,0:T(8,128)(2,1)S(1)}, bf16[8,8,2048]{2,1,0:T(8,128)(2,1)S(1)}, u32[]{:S(2)}, u32[]{:S(2)}) %collective-permute-start.2) | collective-permute-done | bytes 262176 | tf_op jit(solution)/shard_map/ppermute | solution.py:12
  37.4 2.1 %fusion.34 = (f32[512]{0:T(512)S(1)}, f32[128,512]{1,0:T(8,128)S(1)}) fusion(bf16[2048,512]{1,0:T(8,128)(2,1)} %param.15, bf16[16,8,2048]{2,1,0:T(8,128)(2,1)S(1)} %scatter_fusion.2), kind=kOutput, calls=%fused_computation.102 | convolution fusion | flops 268500480 | bytes 2885632 | tf_op jit(solution)/shard_map/dot_general | solution.py:48
  39.5 5.7 %psum.42 = f32[512]{0:T(512)S(1)} all-reduce(f32[512]{0:T(512)S(1)} %get-tuple-element.28), channel_id=1, replica_groups=mesh['dp'=8,'bn'=4] {'bn'}, use_global_device_ids=true, to_apply=%region_8.10 | all-reduce | flops 512 | bytes 4096 | tf_op jit(solution)/shard_map/psum | solution.py:21
  45.2 6.5 %psum.43 = f32[512]{0:T(512)S(1)} all-reduce(f32[512]{0:T(512)S(1)} %multiply_reduce_fusion.2), channel_id=1, replica_groups=mesh['dp'=8,'bn'=4] {'bn'}, use_global_device_ids=true, to_apply=%region_10.12 | all-reduce | flops 512 | bytes 4096 | tf_op jit(solution)/shard_map/psum | solution.py:23
  51.9 1.8 fusion.35
  53.7 5.7 %psum.44 = f32[512]{0:T(512)S(1)} all-reduce(f32[512]{0:T(512)S(1)} %get-tuple-element.30), channel_id=1, replica_groups=mesh['dp'=8,'bn'=4] {'bn'}, use_global_device_ids=true, to_apply=%region_12.14 | all-reduce | flops 512 | bytes 4096 | tf_op jit(solution)/shard_map/psum | solution.py:21
  59.5 6.2 %psum.45 = f32[512]{0:T(512)S(1)} all-reduce(f32[512]{0:T(512)S(1)} %multiply_reduce_fusion.1), channel_id=1, replica_groups=mesh['dp'=8,'bn'=4] {'bn'}, use_global_device_ids=true, to_apply=%region_14.16 | all-reduce | flops 512 | bytes 4096 | tf_op jit(solution)/shard_map/psum | solution.py:23
  67.2 5.9 %psum.46 = f32[2048]{0:T(1024)S(1)} all-reduce(f32[2048]{0:T(1024)S(1)} %get-tuple-element.32), channel_id=1, replica_groups=mesh['dp'=8,'bn'=4] {'bn'}, use_global_device_ids=true, to_apply=%region_16.18 | all-reduce | flops 2048 | bytes 16384 | tf_op jit(solution)/shard_map/psum | solution.py:21
  74.4 6.7 %psum.47 = f32[2048]{0:T(1024)S(1)} all-reduce(f32[2048]{0:T(1024)S(1)} %multiply_reduce_fusion), channel_id=1, replica_groups=mesh['dp'=8,'bn'=4] {'bn'}, use_global_device_ids=true, to_apply=%region_18.20 | all-reduce | flops 2048 | bytes 16384 | tf_op jit(solution)/shard_map/psum | solution.py:23
  81.2 1.7 convert_reduce_fusion
  84.7 2.9 %collective-permute-done.3 = bf16[8,128]{1,0:T(8,128)(2,1)S(1)} collective-permute-done((bf16[8,128]{1,0:T(8,128)(2,1)S(1)}, bf16[8,128]{1,0:T(8,128)(2,1)S(1)}, u32[]{:S(2)}, u32[]{:S(2)}) %collective-permute-start.3) | collective-permute-done | bytes 2080 | tf_op jit(solution)/shard_map/ppermute | solution.py:12
  89.0 3.3 %collective-permute-done.4 = bf16[8,128]{1,0:T(8,128)(2,1)S(1)} collective-permute-done((bf16[8,128]{1,0:T(8,128)(2,1)S(1)}, bf16[8,128]{1,0:T(8,128)(2,1)S(1)}, u32[]{:S(2)}, u32[]{:S(2)}) %collective-permute-start.4) | collective-permute-done | bytes 2080 | tf_op jit(solution)/shard_map/ppermute | solution.py:12
  93.6 1.6 collective-permute-start.5
  96.5 1.6 collective-permute-done.5
  98.7 30.4 %all_gather.6 = bf16[128,128]{1,0:T(8,128)(2,1)S(1)} all-gather(bf16[16,128]{1,0:T(8,128)(2,1)S(1)} %scatter_fusion.5), channel_id=1, replica_groups=mesh['dp'=8,'bn'=4] {'dp'}, dimensions={0}, use_global_device_ids=true | all-gather | bytes 36864 | tf_op jit(solution)/shard_map/all_gather | solution.py:76
  129.9 30.4 %all_gather.7 = bf16[128,128]{1,0:T(8,128)(2,1)S(1)} all-gather(bf16[16,128]{1,0:T(8,128)(2,1)S(1)} %get-tuple-element.14), channel_id=1, replica_groups=mesh['dp'=8,'bn'=4] {'dp'}, dimensions={0}, use_global_device_ids=true | all-gather | bytes 36864 | tf_op jit(solution)/shard_map/all_gather | solution.py:40
  160.3 3.4 %fusion.6 = f32[128]{0:T(128)S(1)} fusion(bf16[128,128]{1,0:T(8,128)(2,1)S(1)} %all_gather.7, bf16[8192,128]{1,0:T(8,128)(2,1)} %param.20, f32[8192]{0:T(1024)S(1)} %add_rsqrt_fusion), kind=kOutput, calls=%fused_computation.21 | convolution fusion | flops 274726784 | bytes 2163200 | tf_op jit(solution)/shard_map/dot_general | solution.py:74
  163.7 21.1 %all-reduce.1 = f32[128]{0:T(128)S(1)} all-reduce(f32[128]{0:T(128)S(1)} %fusion.6), channel_id=2, replica_groups=mesh['dp'=8,'bn'=4] {'dp'}, use_global_device_ids=true, to_apply=%region_27.30.clone | all-reduce | flops 128 | bytes 1024
  (69 shorter events, 20.0 us)
Async XLA Ops:
  0.0 65.7 %copy-start = (bf16[512,2048]{1,0:T(8,128)(2,1)S(1)}, bf16[512,2048]{1,0:T(8,128)(2,1)}, u32[]{:S(2)}) copy-start(bf16[512,2048]{1,0:T(8,128)(2,1)} %param.17) | copy-start | bytes 6291460
  3.8 9.3 %collective-permute-start = (bf16[8,8,2048]{2,1,0:T(8,128)(2,1)S(1)}, bf16[8,8,2048]{2,1,0:T(8,128)(2,1)S(1)}, u32[]{:S(2)}, u32[]{:S(2)}) collective-permute-start(bf16[8,8,2048]{2,1,0:T(8,128)(2,1)S(1)} %broadcast_select_fusion.2), channel_id=1, source_target_pairs={{0,4},{4,0},{8,12},{12,8},{16,20},{20,16},{24,28},{28,24},{1,5},{5... | collective-permute-start | bytes 786440 | tf_op jit(solution)/shard_map/ppermute | solution.py:12
  14.5 11.6 %copy-start.3 = (s32[16]{0:T(128)S(1)}, s32[16]{0:T(128)}, u32[]{:S(2)}) copy-start(s32[16]{0:T(128)} %param.21) | copy-start | bytes 196
  14.5 7.6 %collective-permute-start.1 = (bf16[8,8,2048]{2,1,0:T(8,128)(2,1)S(1)}, bf16[8,8,2048]{2,1,0:T(8,128)(2,1)S(1)}, u32[]{:S(2)}, u32[]{:S(2)}) collective-permute-start(bf16[8,8,2048]{2,1,0:T(8,128)(2,1)S(1)} %broadcast_select_fusion.1), channel_id=1, source_target_pairs={{0,8},{4,12},{8,0},{12,4},{16,24},{20,28},{24,16},{28,20},{1,9},{5... | collective-permute-start | bytes 786440 | tf_op jit(solution)/shard_map/ppermute | solution.py:12
  23.5 13.2 %collective-permute-start.2 = (bf16[8,8,2048]{2,1,0:T(8,128)(2,1)S(1)}, bf16[8,8,2048]{2,1,0:T(8,128)(2,1)S(1)}, u32[]{:S(2)}, u32[]{:S(2)}) collective-permute-start(bf16[8,8,2048]{2,1,0:T(8,128)(2,1)S(1)} %broadcast_select_fusion), channel_id=1, source_target_pairs={{0,16},{4,20},{8,24},{12,28},{16,0},{20,4},{24,8},{28,12},{1,17},{... | collective-permute-start | bytes 786440 | tf_op jit(solution)/shard_map/ppermute | solution.py:12
  67.2 15.7 %copy-start.1 = (bf16[2048,128]{1,0:T(8,128)(2,1)S(1)}, bf16[2048,128]{1,0:T(8,128)(2,1)}, u32[]{:S(2)}) copy-start(bf16[2048,128]{1,0:T(8,128)(2,1)} %param.18) | copy-start | bytes 1572868
  67.2 17.4 %copy-start.2 = (bf16[16,128]{1,0:T(8,128)(2,1)S(1)}, bf16[16,128]{1,0:T(8,128)(2,1)}, u32[]{:S(2)}) copy-start(bf16[16,128]{1,0:T(8,128)(2,1)} %param.19) | copy-start | bytes 12292
  67.2 28.1 %copy-start.4 = (u32[32]{0:T(128)S(1)}, u32[32]{0:T(128)}, u32[]{:S(2)}) copy-start(u32[32]{0:T(128)} %constant.121) | copy-start | bytes 388
  83.9 3.6 %collective-permute-start.3 = (bf16[8,128]{1,0:T(8,128)(2,1)S(1)}, bf16[8,128]{1,0:T(8,128)(2,1)S(1)}, u32[]{:S(2)}, u32[]{:S(2)}) collective-permute-start(bf16[8,128]{1,0:T(8,128)(2,1)S(1)} %broadcast_select_fusion.5), channel_id=1, source_target_pairs={{0,4},{4,0},{8,12},{12,8},{16,20},{20,16},{24,28},{28,24},{1,5},{5... | collective-permute-start | bytes 6152 | tf_op jit(solution)/shard_map/ppermute | solution.py:12
  88.8 3.6 %collective-permute-start.4 = (bf16[8,128]{1,0:T(8,128)(2,1)S(1)}, bf16[8,128]{1,0:T(8,128)(2,1)S(1)}, u32[]{:S(2)}, u32[]{:S(2)}) collective-permute-start(bf16[8,128]{1,0:T(8,128)(2,1)S(1)} %broadcast_select_fusion.4), channel_id=1, source_target_pairs={{0,8},{4,12},{8,0},{12,4},{16,24},{20,28},{24,16},{28,20},{1,9},{5... | collective-permute-start | bytes 6152 | tf_op jit(solution)/shard_map/ppermute | solution.py:12
  93.6 4.5 %collective-permute-start.5 = (bf16[8,128]{1,0:T(8,128)(2,1)S(1)}, bf16[8,128]{1,0:T(8,128)(2,1)S(1)}, u32[]{:S(2)}, u32[]{:S(2)}) collective-permute-start(bf16[8,128]{1,0:T(8,128)(2,1)S(1)} %broadcast_select_fusion.3), channel_id=1, source_target_pairs={{0,16},{4,20},{8,24},{12,28},{16,0},{20,4},{24,8},{28,12},{1,17},{... | collective-permute-start | bytes 6152 | tf_op jit(solution)/shard_map/ppermute | solution.py:12
where the time goes:
time: 186 us; the launch traced here: 185 us
  blocking collectives  119 us (64%)
  waiting for transfers between devices  25 us (13%)
  other arithmetic  12 us (6%)
  starting transfers between devices  9.94 us (5%)
  local copies, waits for them, and re-layouts  9.89 us (5%)
  matrix products  8.99 us (5%)
    all_gather x1, blocking collectives, on_device(): key_all = lax.all_gather(key_unit, 'dp', axis=0, tiled=True)  30.4 us
    all_gather x1, blocking collectives, on_device(): query_all = lax.all_gather(query_unit, 'dp', axis=0, tiled=True)  30.4 us
    ppermute x6, waiting for transfers between devices, partner_2(): lax.ppermute(value, axis, [(i, i ^ 1 << distance) for i in range(lax.axis...  25 us
    unnamed x1, blocking collectives  21.1 us
    psum x3, blocking collectives, group_norm(): lax.psum(jnp.sum(jnp.square(values - center), axis=0), 'bn') / row_total  19.5 us
    psum x3, blocking collectives, group_norm(): first = lax.psum(jnp.sum(values, axis=0), 'bn')  17.2 us
    ppermute x6, starting transfers between devices, partner_2(): lax.ppermute(value, axis, [(i, i ^ 1 << distance) for i in range(lax.axis...  9.94 us
    sort x3, other arithmetic, moving_slots(): return jnp.argsort(1 - flags, stable=True)[:half]  3.74 us
  transfers between devices with their start and end apart: 6, of which 6 were waited for; matrix products, arithmetic and copies ran while one was open for 3% of the time, Pallas kernels for 0%

commit v1 on v0

--- a/solution.py
+++ b/solution.py
@@ -1,6 +1,10 @@
+import functools
+
 import jax
 import jax.numpy as jnp
 from jax import lax
+from jax.experimental import pallas as pl
+from jax.experimental.pallas import tpu as pltpu
 from jax.sharding import PartitionSpec as P
 
 EPS_BN = 1e-05
@@ -29,7 +33,7 @@
     return jnp.argsort(1 - flags, stable=True)[:half]
 
 
-def on_device(features, shuffle_masks, conv_in, conv_mid, conv_out, head, queries, queue, positive):
+def on_device_moving(features, shuffle_masks, conv_in, conv_mid, conv_out, head, queries, queue, positive):
     dp_count = lax.axis_size("dp")
     bn_count = lax.axis_size("bn")
     bit_count = dp_count.bit_length() - 1
@@ -84,9 +88,333 @@
     return jnp.log(jnp.exp(positive_logit - INV_TEMP) + negative) + INV_TEMP - positive_logit
 
 
+MESH = pl.DeviceIdType.MESH
+LANES = 128
+QUEUE_STEPS = 8
+PHASES = ("query", "sum1", "norm1", "sum2", "norm2", "sum3", "norm3", "queue", "key")
+
+
+def fixed_kernel(
+    n_dp, n_bn,
+    masks, positive, queries, x_hbm, in_hbm, mid_hbm, out_hbm, head_hbm, queue_hbm,
+    loss_ref,
+    x_ref, in_ref, mid_ref, out_ref, head_ref, queue_ref,
+    h_ref, wide_ref, mean_ref, scale_ref,
+    send1, recv1, own1, stat1, send2, recv2, own2, stat2, send3, recv3, own3, stat3,
+    query_own, query_all, part_own, part_all, key_own, key_all,
+    load_sem, send_sem, recv_sem,
+):
+    f32, bf16 = jnp.float32, jnp.bfloat16
+    n_dev = n_dp * n_bn
+    d = lax.axis_index("dp")
+    b = lax.axis_index("bn")
+    me = d * n_bn + b
+    rows, channels = x_ref.shape
+    slots = masks.shape[0]
+    cells = rows // slots
+    middle = in_ref.shape[1]
+    total = float(rows * n_bn)
+
+    loads = [
+        pltpu.make_async_copy(src, dst, load_sem.at[i])
+        for i, (src, dst) in enumerate(
+            [(x_hbm, x_ref), (in_hbm, in_ref), (queue_hbm, queue_ref), (mid_hbm, mid_ref), (out_hbm, out_ref), (head_hbm, head_ref)]
+        )
+    ]
+    for load in loads:
+        load.start()
+
+    barrier = pltpu.get_barrier_semaphore()
+
+    def greet(k, carry):
+        t = (me + k) % n_dev
+        pl.semaphore_signal(barrier, inc=1, device_id=(t // n_bn, t % n_bn), device_id_type=MESH)
+        return carry
+
+    lax.fori_loop(1, n_dev, greet, 0)
+
+    lane = lax.broadcasted_iota(jnp.int32, (slots, slots), 1)
+    sub = lax.broadcasted_iota(jnp.int32, (slots, slots), 0)
+    mask_row = jnp.zeros((slots, slots), jnp.int32)
+    mask_col = jnp.zeros((slots, slots), jnp.int32)
+    pos_row = jnp.zeros((1, slots), jnp.int32)
+    lane1 = lax.broadcasted_iota(jnp.int32, (1, slots), 1)
+    groups = []
+    for s in range(slots):
+        groups.append(masks[s] ^ d)
+        mask_row = jnp.where(lane == s, groups[s], mask_row)
+        mask_col = jnp.where(sub == s, groups[s], mask_col)
+        pos_row = jnp.where(lane1 == s, positive[s], pos_row)
+    same = (mask_row == mask_col).astype(f32)
+    local_mean = same / (jnp.sum(same, axis=0, keepdims=True) * float(cells))
+    member = (mask_row[:n_dp] == sub[:n_dp]).astype(f32) if n_dp <= slots else None
+    counts = []
+    for e in range(n_dp):
+        want = e ^ d
+        count = jnp.int32(0)
+        for s in range(slots):
+            count = count + (masks[s] == want).astype(jnp.int32)
+        counts.append((count * cells).astype(f32))
+
+    q = queries[...].astype(f32)
+    query_unit = (q * lax.rsqrt(jnp.sum(q * q, axis=-1, keepdims=True) + EPS_UNIT)).astype(bf16)
+    query_own[...] = query_unit
+    query_all[d] = query_unit
+
+    pl.semaphore_wait(barrier, n_dev - 1)
+
+    def all_peers(phase, src_of, dst):
+        i = PHASES.index(phase)
+
+        def step(k, carry):
+            t = (me + k) % n_dev
+            pltpu.make_async_remote_copy(
+                src_ref=src_of(t // n_bn, t % n_bn), dst_ref=dst.at[me],
+                send_sem=send_sem.at[i], recv_sem=recv_sem.at[i],
+                device_id=(t // n_bn, t % n_bn), device_id_type=MESH,
+            ).start()
+            return carry
+
+        lax.fori_loop(1, n_dev, step, 0)
+
+    def column_peers(phase, src, dst):
+        i = PHASES.index(phase)
+
+        def step(k, carry):
+            t = (d + k) % n_dp
+            pltpu.make_async_remote_copy(
+                src_ref=src, dst_ref=dst.at[d],
+                send_sem=send_sem.at[i], recv_sem=recv_sem.at[i],
+                device_id=(t, b), device_id_type=MESH,
+            ).start()
+            return carry
+
+        lax.fori_loop(1, n_dp, step, 0)
+
+    def arrived(phase, dst):
+        most = dst.at[pl.ds(0, dst.shape[0] - 1)]
+        pltpu.make_async_copy(most, most, recv_sem.at[PHASES.index(phase)]).wait()
+
+    def sent(phase, dst):
+        most = dst.at[pl.ds(0, dst.shape[0] - 1)]
+        pltpu.make_async_copy(most, most, send_sem.at[PHASES.index(phase)]).wait()
+
+    def exact(a, c):
+        return jnp.dot(a, c, preferred_element_type=f32, precision=lax.Precision.HIGHEST)
+
+    def send_sums(phase, h, send, recv):
+        width = h.shape[1]
+        block = width // n_bn
+        subs = block // LANES
+        shaped = h.reshape(slots, cells, width)
+        sums = jnp.sum(shaped, axis=1)
+        center = exact(local_mean, sums)
+        squares = jnp.sum(jnp.square(shaped - center[:, None, :]), axis=1)
+        for at, values in ((0, exact(member, sums)), (subs, exact(member, squares))):
+            for j in range(n_bn):
+                for r in range(subs):
+                    low = j * block + r * LANES
+                    send[:, j, at + r, :] = values[:, low : low + LANES]
+        recv[me] = send[d, b]
+        all_peers(phase, lambda g, j: send.at[g, j], recv)
+
+    def send_norm(phase_in, phase_out, recv, own, stat):
+        arrived(phase_in, recv)
+        subs = recv.shape[1] // 2
+        both = jnp.sum(recv[...], axis=0)
+        mean = both[:subs] * (1.0 / total)
+        spread = both[subs:]
+        for e in range(n_dp):
+            part = recv[e * n_bn : (e + 1) * n_bn][:, :subs]
+            off = jnp.sum(jnp.square(part - counts[e] * mean[None]), axis=0)
+            spread = spread + off / jnp.maximum(counts[e], 1.0)
+        own[:subs] = mean
+        own[subs:] = lax.rsqrt(spread * (1.0 / total) + EPS_BN)
+        stat[me] = own[...]
+        all_peers(phase_out, lambda g, j: own, stat)
+
+    def tables(phase, stat, width):
+        arrived(phase, stat)
+        block = width // n_bn
+        subs = block // LANES
+        held = stat[...].reshape(n_dp, n_bn, 2 * subs, LANES)
+        for j in range(n_bn):
+            for r in range(subs):
+                low = j * block + r * LANES
+                mean_ref[:, low : low + LANES] = held[:, j, r, :]
+                scale_ref[:, low : low + LANES] = held[:, j, subs + r, :]
+
+    def slot_row(table, s, width):
+        return jnp.broadcast_to(table[pl.ds(groups[s], 1), :width], (cells, width))
+
+    ones = jnp.ones((LANES, LANES), bf16)
+    step_rows = queue_ref.shape[0] // QUEUE_STEPS
+
+    def queue_step(c, total_part):
+        raw = queue_ref[pl.ds(c * step_rows, step_rows), :].astype(f32)
+        square = raw * raw
+        high = square.astype(bf16)
+        low = (square - high.astype(f32)).astype(bf16)
+        norm = jnp.dot(high, ones, preferred_element_type=f32) + jnp.dot(low, ones, preferred_element_type=f32)
+        unit = (raw * lax.rsqrt(norm + EPS_UNIT)).astype(bf16)
+        flat_queries = query_all[...].reshape(n_dp * slots, query_all.shape[2])
+        scores = lax.dot_general(unit, flat_queries, (((1,), (1,)), ((), ())), preferred_element_type=f32)
+        terms = jnp.exp(scores * INV_TEMP - INV_TEMP)
+        return total_part + jnp.sum(terms.reshape(step_rows // 8, 8, n_dp * slots), axis=0)
+
+    def queue_steps(first, last, total_part):
+        return lax.fori_loop(first, last, queue_step, total_part)
+
+    column_peers("query", query_own, query_all)
+
+    loads[0].wait()
+    loads[1].wait()
+    h_ref[...] = jnp.dot(x_ref[...], in_ref[...], preferred_element_type=f32)
+    send_sums("sum1", h_ref[...], send1, recv1)
+    part = jnp.zeros((8, n_dp * slots), f32)
+    loads[2].wait()
+    arrived("query", query_all)
+    part = queue_steps(0, 2, part)
+    send_norm("sum1", "norm1", recv1, own1, stat1)
+    loads[3].wait()
+    part = queue_steps(2, 3, part)
+    tables("norm1", stat1, middle)
+
+    for s in range(slots):
+        at = slice(s * cells, (s + 1) * cells)
+        h_ref[at] = jax.nn.relu((h_ref[at] - slot_row(mean_ref, s, middle)) * slot_row(scale_ref, s, middle))
+    act = h_ref[...]
+    cell = lax.broadcasted_iota(jnp.int32, act.shape, 0) % cells
+    before = jnp.where(cell == 0, 0.0, pltpu.roll(act, 1, 0)).astype(bf16)
+    after = jnp.where(cell == cells - 1, 0.0, pltpu.roll(act, rows - 1, 0)).astype(bf16)
+    h_ref[...] = (
+        jnp.dot(before, mid_ref[0], preferred_element_type=f32)
+        + jnp.dot(act.astype(bf16), mid_ref[1], preferred_element_type=f32)
+        + jnp.dot(after, mid_ref[2], preferred_element_type=f32)
+    )
+    send_sums("sum2", h_ref[...], send2, recv2)
+    part = queue_steps(3, 5, part)
+    send_norm("sum2", "norm2", recv2, own2, stat2)
+    loads[4].wait()
+    part = queue_steps(5, 6, part)
+    tables("norm2", stat2, middle)
+
+    for s in range(slots):
+        at = slice(s * cells, (s + 1) * cells)
+        h_ref[at] = jax.nn.relu((h_ref[at] - slot_row(mean_ref, s, middle)) * slot_row(scale_ref, s, middle))
+    wide_ref[...] = jnp.dot(h_ref[...].astype(bf16), out_ref[...], preferred_element_type=f32)
+    send_sums("sum3", wide_ref[...], send3, recv3)
+    part = queue_steps(6, 8, part)
+    part_own[...] = jnp.sum(part, axis=0, keepdims=True)
+    part_all[d] = part_own[...]
+    column_peers("queue", part_own, part_all)
+    send_norm("sum3", "norm3", recv3, own3, stat3)
+    loads[5].wait()
+    tables("norm3", stat3, channels)
+
+    pooled = []
+    for i in range(slots // 2):
+        at = slice(2 * i * cells, (2 * i + 2) * cells)
+        mean = jnp.concatenate([slot_row(mean_ref, 2 * i + o, channels) for o in range(2)], axis=0)
+        scale = jnp.concatenate([slot_row(scale_ref, 2 * i + o, channels) for o in range(2)], axis=0)
+        block = jax.nn.relu((wide_ref[at] - mean) * scale + x_ref[at].astype(f32)).astype(bf16)
+        pooled.append(jnp.mean(block.astype(f32).reshape(2, cells, channels), axis=1))
+    pooled = jnp.concatenate(pooled, axis=0).astype(bf16)
+    z = jnp.dot(pooled, head_ref[...], preferred_element_type=f32)
+    key_own[...] = (z * lax.rsqrt(jnp.sum(z * z, axis=-1, keepdims=True) + EPS_UNIT)).astype(bf16)
+    key_all[d] = key_own[...]
+    column_peers("key", key_own, key_all)
+
+    arrived("queue", part_all)
+    negative_all = jnp.sum(part_all[...], axis=0)
+    mine = lax.broadcasted_iota(jnp.int32, (slots, n_dp * slots), 1) == (
+        lax.broadcasted_iota(jnp.int32, (slots, n_dp * slots), 0) + d * slots
+    )
+    negative_col = jnp.sum(jnp.where(mine, negative_all, 0.0), axis=1, keepdims=True)
+    negative = jnp.sum(jnp.where(lane == sub, negative_col, 0.0), axis=0, keepdims=True)
+    want = (pos_row // (slots * n_bn)) * slots + pos_row % slots
+
+    arrived("key", key_all)
+    keys = key_all[...].reshape(n_dp * slots, key_all.shape[2])
+    pairs = lax.dot_general(keys, query_own[...], (((1,), (1,)), ((), ())), preferred_element_type=f32)
+    chosen = lax.broadcasted_iota(jnp.int32, pairs.shape, 0) == want
+    logit = jnp.sum(jnp.where(chosen, pairs, 0.0), axis=0, keepdims=True) * INV_TEMP
+    loss_ref[...] = jnp.log(jnp.exp(logit - INV_TEMP) + negative) + INV_TEMP - logit
+
+    for phase, dst in zip(PHASES, (query_all, recv1, stat1, recv2, stat2, recv3, stat3, part_all, key_all)):
+        sent(phase, dst)
+
+
+def on_device_fixed(n_dp, n_bn, features, shuffle_masks, conv_in, conv_mid, conv_out, head, queries, queue, positive):
+    f32, bf16 = jnp.float32, jnp.bfloat16
+    slots, cells, channels = features.shape
+    rows = slots * cells
+    middle = conv_in.shape[1]
+    width = queries.shape[1]
+    n_dev = n_dp * n_bn
+
+    def exchange(c):
+        tile = (2 * (c // n_bn // LANES), LANES)
+        return [
+            pltpu.VMEM((n_dp, n_bn) + tile, f32),
+            pltpu.VMEM((n_dev,) + tile, f32),
+            pltpu.VMEM(tile, f32),
+            pltpu.VMEM((n_dev,) + tile, f32),
+        ]
+
+    smem = pl.BlockSpec(memory_space=pltpu.SMEM)
+    vmem = pl.BlockSpec(memory_space=pltpu.VMEM)
+    hbm = pl.BlockSpec(memory_space=pl.ANY)
+    loss = pl.pallas_call(
+        functools.partial(fixed_kernel, n_dp, n_bn),
+        out_shape=jax.ShapeDtypeStruct((1, slots), f32),
+        in_specs=[smem, smem, vmem] + [hbm] * 6,
+        out_specs=vmem,
+        scratch_shapes=[
+            pltpu.VMEM((rows, channels), bf16),
+            pltpu.VMEM(conv_in.shape, bf16),
+            pltpu.VMEM(conv_mid.shape, bf16),
+            pltpu.VMEM(conv_out.shape, bf16),
+            pltpu.VMEM(head.shape, bf16),
+            pltpu.VMEM(queue.shape, bf16),
+            pltpu.VMEM((rows, middle), f32),
+            pltpu.VMEM((rows, channels), f32),
+            pltpu.VMEM((n_dp, channels), f32),
+            pltpu.VMEM((n_dp, channels), f32),
+        ]
+        + exchange(middle)
+        + exchange(middle)
+        + exchange(channels)
+        + [
+            pltpu.VMEM((slots, width), bf16),
+            pltpu.VMEM((n_dp, slots, width), bf16),
+            pltpu.VMEM((1, n_dp * slots), f32),
+            pltpu.VMEM((n_dp, 1, n_dp * slots), f32),
+            pltpu.VMEM((slots, width), bf16),
+            pltpu.VMEM((n_dp, slots, width), bf16),
+            pltpu.SemaphoreType.DMA((6,)),
+            pltpu.SemaphoreType.DMA((len(PHASES),)),
+            pltpu.SemaphoreType.DMA((len(PHASES),)),
+        ],
+        compiler_params=pltpu.CompilerParams(
+            collective_id=0, has_side_effects=True, vmem_limit_bytes=48 << 20
+        ),
+        name="fixed_crops",
+    )(shuffle_masks, positive, queries, features.reshape(rows, channels), conv_in, conv_mid, conv_out, head, queue)
+    return loss.reshape(slots)
+
+
+def on_device(n_dp, n_bn, *arrays):
+    features, conv_in = arrays[0], arrays[2]
+    whole_lanes = conv_in.shape[1] % (n_bn * LANES) == 0 and features.shape[2] % (n_bn * LANES) == 0
+    if whole_lanes and n_dp <= features.shape[0] and features.shape[1] == 8:
+        return on_device_fixed(n_dp, n_bn, *arrays)
+    return on_device_moving(*arrays)
+
+
 def solution(mesh):
     return jax.shard_map(
-        on_device,
+        functools.partial(on_device, mesh.shape["dp"], mesh.shape["bn"]),
         mesh=mesh,
         in_specs=(
             P(("dp", "bn"), None, None),

time: 186 us -> 54.4 us (0.29)
  blocking collectives: 119 us -> 0 us
  Pallas kernels: 0 us -> 46.5 us
  waiting for transfers between devices: 25 us -> 0 us
  other arithmetic: 12 us -> 0 us
  starting transfers between devices: 9.94 us -> 0 us
  matrix products: 8.99 us -> 0 us
  local copies, waits for them, and re-layouts: 9.89 us -> 7.59 us
    all_gather x2 -> x0, blocking collectives: 60.8 us -> none  [the longest x1 30.4 us: on_device(): key_all = lax.all_gather(key_unit, 'dp', axis=0, tiled=True)]
    pallas_call x0 -> x1, Pallas kernels: none -> 46.5 us  [on_device_fixed(): pl.pallas_call(functools.partial(fixed_kernel, n_dp, n_bn), out_shape=jax...]
    psum x6 -> x0, blocking collectives: 36.7 us -> none  [the longest x3 19.5 us: group_norm(): lax.psum(jnp.sum(jnp.square(values - center), axis=0), 'bn') / row_total]
    ppermute x6 -> x0, waiting for transfers between devices: 25 us -> none  [partner_2(): lax.ppermute(value, axis, [(i, i ^ 1 << distance) for i in range(lax.axis...]
    unnamed x1 -> x0, blocking collectives: 21.1 us -> none
    ppermute x6 -> x0, starting transfers between devices: 9.94 us -> none  [partner_2(): lax.ppermute(value, axis, [(i, i ^ 1 << distance) for i in range(lax.axis...]
    dot_general x5 -> x0, matrix products: 8.99 us -> none  [the longest x1 3.36 us: on_device(): jnp.dot(query_all, queue_unit.T, preferred_element_type=jnp.float32)]
    reduce_sum x7 -> x0, other arithmetic: 6.21 us -> none  [the longest x2 2.86 us: unit_rows(): jnp.sum(values * values, axis=-1, keepdims=True) + EPS_UNIT]
  transfers between devices with their start and end apart: 6 -> 0, of which waited for: 6 -> 0; matrix products, arithmetic and copies ran while one was open for 3% -> 0% of each run, Pallas kernels for 0% -> 0%
where the time goes in v1:
time: 54.4 us; the launch traced here: 54.1 us
  Pallas kernels  46.5 us (85%)
  local copies, waits for them, and re-layouts  7.59 us (14%)
    pallas_call x1, Pallas kernels, on_device_fixed(): pl.pallas_call(functools.partial(fixed_kernel, n_dp, n_bn), out_shape=jax...  46.5 us
    unnamed x15, local copies, waits for them, and re-layouts  7.59 us

profile of v1, /device:TPU:0, one launch (start us, length us, event | category | flops | bytes accessed | tf_op | source)
XLA Modules:
  0.0 54.1 jit_solution(12280289078783721250)
XLA Ops:
  0.0 0.0 copy-start
  0.0 1.6 %copy-done = bf16[2048,512]{1,0:T(8,128)(2,1)S(1)} copy-done((bf16[2048,512]{1,0:T(8,128)(2,1)S(1)}, bf16[2048,512]{1,0:T(8,128)(2,1)}, u32[]{:S(2)}) %copy-start) | copy-done | bytes 2097176
  1.6 0.0 copy-start.1
  1.6 1.4 %copy-done.1 = bf16[3,512,512]{2,1,0:T(8,128)(2,1)S(1)} copy-done((bf16[3,512,512]{2,1,0:T(8,128)(2,1)S(1)}, bf16[3,512,512]{2,1,0:T(8,128)(2,1)}, u32[]{:S(2)}) %copy-start.1) | copy-done | bytes 1572888
  3.0 0.0 copy-start.2
  3.0 1.0 %copy-done.2 = bf16[16,8,2048]{2,1,0:T(8,128)(2,1)S(1)} copy-done((bf16[16,8,2048]{2,1,0:T(8,128)(2,1)S(1)}, bf16[16,8,2048]{2,1,0:T(8,128)(2,1)}, u32[]{:S(2)}) %copy-start.2) | copy-done | bytes 524312
  4.0 0.0 copy-start.3
  4.0 1.0 %copy-done.3 = bf16[2048,128]{1,0:T(8,128)(2,1)S(1)} copy-done((bf16[2048,128]{1,0:T(8,128)(2,1)S(1)}, bf16[2048,128]{1,0:T(8,128)(2,1)}, u32[]{:S(2)}) %copy-start.3) | copy-done | bytes 524312
  5.1 0.0 copy-start.4
  5.1 0.7 %copy-done.4 = bf16[16,128]{1,0:T(8,128)(2,1)S(1)} copy-done((bf16[16,128]{1,0:T(8,128)(2,1)S(1)}, bf16[16,128]{1,0:T(8,128)(2,1)}, u32[]{:S(2)}) %copy-start.4) | copy-done | bytes 4120
  5.8 0.0 copy-start.5
  5.8 0.7 %copy-done.5 = s32[16]{0:T(128)S(1)} copy-done((s32[16]{0:T(128)S(1)}, s32[16]{0:T(128)}, u32[]{:S(2)}) %copy-start.5) | copy-done | bytes 88
  6.4 0.0 copy-start.6
  6.4 0.7 %copy-done.6 = s32[16]{0:T(128)S(1)} copy-done((s32[16]{0:T(128)S(1)}, s32[16]{0:T(128)}, u32[]{:S(2)}) %copy-start.6) | copy-done | bytes 88
  7.1 46.5 %fixed_crops.1 = f32[1,16]{1,0:T(1,128)S(1)} custom-call(s32[16]{0:T(128)S(1)} %copy-done.5, s32[16]{0:T(128)S(1)} %copy-done.6, bf16[16,128]{1,0:T(8,128)(2,1)S(1)} %copy-done.4, bf16[128,2048]{1,0:T(8,128)(2,1)S(1)} %bitcast.2, bf16[2048,512]{1,0:T(8,128)(2,1)S(1)} %copy-done, bf16[3,512,512]{2,1,0:T(8,128)(2,1)S(1)} %copy-done.1, ...), custom_call_target="tpu_custom_call" | custom-call | tf_op jit(solution)/shard_map/fixed_crops/pallas_call | solution.py:368
  53.6 0.5 copy.11
Async XLA Ops:
  0.0 1.6 %copy-start = (bf16[2048,512]{1,0:T(8,128)(2,1)S(1)}, bf16[2048,512]{1,0:T(8,128)(2,1)}, u32[]{:S(2)}) copy-start(bf16[2048,512]{1,0:T(8,128)(2,1)} %in_hbm.1) | copy-start | bytes 6291460
  1.6 1.4 %copy-start.1 = (bf16[3,512,512]{2,1,0:T(8,128)(2,1)S(1)}, bf16[3,512,512]{2,1,0:T(8,128)(2,1)}, u32[]{:S(2)}) copy-start(bf16[3,512,512]{2,1,0:T(8,128)(2,1)} %mid_hbm.1) | copy-start | bytes 4718596
  3.0 1.0 %copy-start.2 = (bf16[16,8,2048]{2,1,0:T(8,128)(2,1)S(1)}, bf16[16,8,2048]{2,1,0:T(8,128)(2,1)}, u32[]{:S(2)}) copy-start(bf16[16,8,2048]{2,1,0:T(8,128)(2,1)} %param.9) | copy-start | bytes 1572868
  4.0 1.0 %copy-start.3 = (bf16[2048,128]{1,0:T(8,128)(2,1)S(1)}, bf16[2048,128]{1,0:T(8,128)(2,1)}, u32[]{:S(2)}) copy-start(bf16[2048,128]{1,0:T(8,128)(2,1)} %head_hbm.1) | copy-start | bytes 1572868
  5.1 0.7 %copy-start.4 = (bf16[16,128]{1,0:T(8,128)(2,1)S(1)}, bf16[16,128]{1,0:T(8,128)(2,1)}, u32[]{:S(2)}) copy-start(bf16[16,128]{1,0:T(8,128)(2,1)} %queries.1) | copy-start | bytes 12292
  5.8 0.7 %copy-start.5 = (s32[16]{0:T(128)S(1)}, s32[16]{0:T(128)}, u32[]{:S(2)}) copy-start(s32[16]{0:T(128)} %masks.1) | copy-start | bytes 196
  6.4 0.7 %copy-start.6 = (s32[16]{0:T(128)S(1)}, s32[16]{0:T(128)}, u32[]{:S(2)}) copy-start(s32[16]{0:T(128)} %positive.1) | copy-start | bytes 196

commit v2 on v1

--- a/solution.py
+++ b/solution.py
@@ -91,18 +91,20 @@
 MESH = pl.DeviceIdType.MESH
 LANES = 128
 QUEUE_STEPS = 8
+PANELS = 4
 PHASES = ("query", "sum1", "norm1", "sum2", "norm2", "sum3", "norm3", "queue", "key")
 
 
 def fixed_kernel(
     n_dp, n_bn,
-    masks, positive, queries, x_hbm, in_hbm, mid_hbm, out_hbm, head_hbm, queue_hbm,
+    masks_hbm, positive_hbm, queries_hbm, x_hbm, in_hbm, mid_hbm, out_hbm, head_hbm, queue_hbm,
     loss_ref,
+    masks, positive, queries,
     x_ref, in_ref, mid_ref, out_ref, head_ref, queue_ref,
     h_ref, wide_ref, mean_ref, scale_ref,
     send1, recv1, own1, stat1, send2, recv2, own2, stat2, send3, recv3, own3, stat3,
     query_own, query_all, part_own, part_all, key_own, key_all,
-    load_sem, send_sem, recv_sem,
+    load_sem, panel_sem, send_sem, recv_sem,
 ):
     f32, bf16 = jnp.float32, jnp.bfloat16
     n_dev = n_dp * n_bn
@@ -115,24 +117,32 @@
     middle = in_ref.shape[1]
     total = float(rows * n_bn)
 
+    panel = channels // PANELS
+    panels = [
+        pltpu.make_async_copy(
+            in_hbm.at[pl.ds(i * panel, panel)], in_ref.at[pl.ds(i * panel, panel)], panel_sem.at[i]
+        )
+        for i in range(PANELS)
+    ]
     loads = [
         pltpu.make_async_copy(src, dst, load_sem.at[i])
         for i, (src, dst) in enumerate(
-            [(x_hbm, x_ref), (in_hbm, in_ref), (queue_hbm, queue_ref), (mid_hbm, mid_ref), (out_hbm, out_ref), (head_hbm, head_ref)]
+            [(masks_hbm, masks), (positive_hbm, positive), (queries_hbm, queries), (x_hbm, x_ref), (queue_hbm, queue_ref), (mid_hbm, mid_ref), (out_hbm, out_ref), (head_hbm, head_ref)]
         )
     ]
-    for load in loads:
+    for load in loads[:4] + panels:
         load.start()
 
     barrier = pltpu.get_barrier_semaphore()
 
-    def greet(k, carry):
-        t = (me + k) % n_dev
-        pl.semaphore_signal(barrier, inc=1, device_id=(t // n_bn, t % n_bn), device_id_type=MESH)
-        return carry
-
-    lax.fori_loop(1, n_dev, greet, 0)
-
+    dps = [lax.rem(d + k, n_dp) for k in range(n_dp)]
+    bns = [lax.rem(b + k, n_bn) for k in range(n_bn)]
+    peers = [(g, j) for g in dps for j in bns][1:]
+    for peer in peers:
+        pl.semaphore_signal(barrier, inc=1, device_id=peer, device_id_type=MESH)
+
+    for load in loads[:3]:
+        load.wait()
     lane = lax.broadcasted_iota(jnp.int32, (slots, slots), 1)
     sub = lax.broadcasted_iota(jnp.int32, (slots, slots), 0)
     mask_row = jnp.zeros((slots, slots), jnp.int32)
@@ -161,35 +171,25 @@
     query_own[...] = query_unit
     query_all[d] = query_unit
 
-    pl.semaphore_wait(barrier, n_dev - 1)
-
     def all_peers(phase, src_of, dst):
         i = PHASES.index(phase)
 
-        def step(k, carry):
-            t = (me + k) % n_dev
+        for g, j in peers:
             pltpu.make_async_remote_copy(
-                src_ref=src_of(t // n_bn, t % n_bn), dst_ref=dst.at[me],
+                src_ref=src_of(g, j), dst_ref=dst.at[me],
                 send_sem=send_sem.at[i], recv_sem=recv_sem.at[i],
-                device_id=(t // n_bn, t % n_bn), device_id_type=MESH,
+                device_id=(g, j), device_id_type=MESH,
             ).start()
-            return carry
-
-        lax.fori_loop(1, n_dev, step, 0)
 
     def column_peers(phase, src, dst):
         i = PHASES.index(phase)
 
-        def step(k, carry):
-            t = (d + k) % n_dp
+        for g in dps[1:]:
             pltpu.make_async_remote_copy(
                 src_ref=src, dst_ref=dst.at[d],
                 send_sem=send_sem.at[i], recv_sem=recv_sem.at[i],
-                device_id=(t, b), device_id_type=MESH,
+                device_id=(g, b), device_id_type=MESH,
             ).start()
-            return carry
-
-        lax.fori_loop(1, n_dp, step, 0)
 
     def arrived(phase, dst):
         most = dst.at[pl.ds(0, dst.shape[0] - 1)]
@@ -265,18 +265,26 @@
     def queue_steps(first, last, total_part):
         return lax.fori_loop(first, last, queue_step, total_part)
 
+    loads[3].wait()
+    first = None
+    for i in range(PANELS):
+        panels[i].wait()
+        at = slice(i * panel, (i + 1) * panel)
+        term = jnp.dot(x_ref[:, at], in_ref[at], preferred_element_type=f32)
+        first = term if first is None else first + term
+        if i == 0:
+            for load in loads[4:]:
+                load.start()
+    h_ref[...] = first
+    pl.semaphore_wait(barrier, n_dev - 1)
     column_peers("query", query_own, query_all)
-
-    loads[0].wait()
-    loads[1].wait()
-    h_ref[...] = jnp.dot(x_ref[...], in_ref[...], preferred_element_type=f32)
     send_sums("sum1", h_ref[...], send1, recv1)
     part = jnp.zeros((8, n_dp * slots), f32)
-    loads[2].wait()
+    loads[4].wait()
     arrived("query", query_all)
     part = queue_steps(0, 2, part)
     send_norm("sum1", "norm1", recv1, own1, stat1)
-    loads[3].wait()
+    loads[5].wait()
     part = queue_steps(2, 3, part)
     tables("norm1", stat1, middle)
 
@@ -295,7 +303,7 @@
     send_sums("sum2", h_ref[...], send2, recv2)
     part = queue_steps(3, 5, part)
     send_norm("sum2", "norm2", recv2, own2, stat2)
-    loads[4].wait()
+    loads[6].wait()
     part = queue_steps(5, 6, part)
     tables("norm2", stat2, middle)
 
@@ -309,7 +317,7 @@
     part_all[d] = part_own[...]
     column_peers("queue", part_own, part_all)
     send_norm("sum3", "norm3", recv3, own3, stat3)
-    loads[5].wait()
+    loads[7].wait()
     tables("norm3", stat3, channels)
 
     pooled = []
@@ -362,15 +370,17 @@
             pltpu.VMEM((n_dev,) + tile, f32),
         ]
 
-    smem = pl.BlockSpec(memory_space=pltpu.SMEM)
     vmem = pl.BlockSpec(memory_space=pltpu.VMEM)
-    hbm = pl.BlockSpec(memory_space=pl.ANY)
+    hbm = pl.BlockSpec(memory_space=pltpu.HBM)
     loss = pl.pallas_call(
         functools.partial(fixed_kernel, n_dp, n_bn),
         out_shape=jax.ShapeDtypeStruct((1, slots), f32),
-        in_specs=[smem, smem, vmem] + [hbm] * 6,
+        in_specs=[hbm] * 9,
         out_specs=vmem,
         scratch_shapes=[
+            pltpu.SMEM(shuffle_masks.shape, jnp.int32),
+            pltpu.SMEM(positive.shape, jnp.int32),
+            pltpu.VMEM(queries.shape, bf16),
             pltpu.VMEM((rows, channels), bf16),
             pltpu.VMEM(conv_in.shape, bf16),
             pltpu.VMEM(conv_mid.shape, bf16),
@@ -392,12 +402,13 @@
             pltpu.VMEM((n_dp, 1, n_dp * slots), f32),
             pltpu.VMEM((slots, width), bf16),
             pltpu.VMEM((n_dp, slots, width), bf16),
-            pltpu.SemaphoreType.DMA((6,)),
+            pltpu.SemaphoreType.DMA((8,)),
+            pltpu.SemaphoreType.DMA((PANELS,)),
             pltpu.SemaphoreType.DMA((len(PHASES),)),
             pltpu.SemaphoreType.DMA((len(PHASES),)),
         ],
         compiler_params=pltpu.CompilerParams(
-            collective_id=0, has_side_effects=True, vmem_limit_bytes=48 << 20
+            collective_id=0, has_side_effects=True, vmem_limit_bytes=64 << 20
         ),
         name="fixed_crops",
     )(shuffle_masks, positive, queries, features.reshape(rows, channels), conv_in, conv_mid, conv_out, head, queue)

time: 54.4 us -> 45.9 us (0.84)
  local copies, waits for them, and re-layouts: 7.59 us -> 1.19 us
  Pallas kernels: 46.5 us -> 44.6 us
    unnamed x15 -> x1, local copies, waits for them, and re-layouts: 7.59 us -> 1.19 us
    pallas_call x1, Pallas kernels: 46.5 us -> 44.6 us  [on_device_fixed(): pl.pallas_call(functools.partial(fixed_kernel, n_dp, n_bn), out_shape=jax...]
where the time goes in v2:
time: 45.9 us; the launch traced here: 45.8 us
  Pallas kernels  44.6 us (97%)
  local copies, waits for them, and re-layouts  1.19 us (3%)
    pallas_call x1, Pallas kernels, on_device_fixed(): pl.pallas_call(functools.partial(fixed_kernel, n_dp, n_bn), out_shape=jax...  44.6 us
    unnamed x1, local copies, waits for them, and re-layouts  1.19 us

profile of v2, /device:TPU:0, one launch (start us, length us, event | category | flops | bytes accessed | tf_op | source)
XLA Modules:
  0.0 45.8 jit_solution(16915269437146363671)
XLA Ops:
  0.0 44.6 %fixed_crops.1 = f32[1,16]{1,0:T(1,128)} custom-call(s32[16]{0:T(128)} %masks_hbm.1, s32[16]{0:T(128)} %positive_hbm.1, bf16[16,128]{1,0:T(8,128)(2,1)} %queries_hbm.1, bf16[128,2048]{1,0:T(8,128)(2,1)} %bitcast.2, bf16[2048,512]{1,0:T(8,128)(2,1)} %in_hbm.1, bf16[3,512,512]{2,1,0:T(8,128)(2,1)} %mid_hbm.1, bf16[512,2048]{1,0:T(8,128)(2,1)} %out_hbm.1, ...), custom_call_target="tpu_custom_call" | custom-call | tf_op jit(solution)/shard_map/fixed_crops/pallas_call | solution.py:375
  44.6 1.2 %copy.11 = f32[16]{0:T(128)} copy(f32[16]{0:T(128)} %bitcast.3) | data formatting | bytes 128

commit v3 on v2

--- a/solution.py
+++ b/solution.py
@@ -104,7 +104,7 @@
     h_ref, wide_ref, mean_ref, scale_ref,
     send1, recv1, own1, stat1, send2, recv2, own2, stat2, send3, recv3, own3, stat3,
     query_own, query_all, part_own, part_all, key_own, key_all,
-    load_sem, panel_sem, send_sem, recv_sem,
+    load_sem, panel_sem, send_sem, recv_sem, ready_sem,
 ):
     f32, bf16 = jnp.float32, jnp.bfloat16
     n_dev = n_dp * n_bn
@@ -137,9 +137,16 @@
 
     dps = [lax.rem(d + k, n_dp) for k in range(n_dp)]
     bns = [lax.rem(b + k, n_bn) for k in range(n_bn)]
-    peers = [(g, j) for g in dps for j in bns][1:]
-    for peer in peers:
+    order = [k for k in (n_dp // 2 + i * o for i in range(n_dp // 2) for o in (1, -1))]
+    order = list(dict.fromkeys(order + list(range(n_dp))))
+    peers = [(dps[k % n_dp], j) for k in order if k % n_dp for j in bns] + [(d, j) for j in bns[1:]]
+    for peer in [(g, b) for g in dps[1:]] + [(d, j) for j in bns[1:]]:
         pl.semaphore_signal(barrier, inc=1, device_id=peer, device_id_type=MESH)
+
+    n_own = n_dev // 2
+    base = n_own // 2
+    owner = jnp.logical_and(me >= base, me < base + n_own)
+    mine_at = jnp.clip(me - base, 0, n_own - 1)
 
     for load in loads[:3]:
         load.wait()
@@ -160,7 +167,7 @@
     member = (mask_row[:n_dp] == sub[:n_dp]).astype(f32) if n_dp <= slots else None
     counts = []
     for e in range(n_dp):
-        want = e ^ d
+        want = e ^ lax.div(2 * mine_at, n_bn)
         count = jnp.int32(0)
         for s in range(slots):
             count = count + (masks[s] == want).astype(jnp.int32)
@@ -171,15 +178,41 @@
     query_own[...] = query_unit
     query_all[d] = query_unit
 
-    def all_peers(phase, src_of, dst):
+    def push(phase, src, dst, peer):
         i = PHASES.index(phase)
-
-        for g, j in peers:
-            pltpu.make_async_remote_copy(
-                src_ref=src_of(g, j), dst_ref=dst.at[me],
-                send_sem=send_sem.at[i], recv_sem=recv_sem.at[i],
-                device_id=(g, j), device_id_type=MESH,
-            ).start()
+        pltpu.make_async_remote_copy(
+            src_ref=src, dst_ref=dst, send_sem=send_sem.at[i], recv_sem=recv_sem.at[i],
+            device_id=peer, device_id_type=MESH,
+        ).start()
+
+    def to_owners(phase, send, recv):
+        for k in range(1, n_own + 1):
+            o = lax.rem(me + k, n_own)
+            t = o + base
+            peer = (lax.div(t, n_bn), lax.rem(t, n_bn))
+            if k == n_own - base:
+                @pl.when(jnp.logical_not(owner))
+                def _():
+                    push(phase, send.at[o], recv.at[me], peer)
+            else:
+                push(phase, send.at[o], recv.at[me], peer)
+
+        @pl.when(owner)
+        def _():
+            recv[me] = send[mine_at]
+
+    def took(sem, ref, n):
+        most = ref.at[pl.ds(0, n)]
+        pltpu.make_async_copy(most, most, sem).wait()
+
+    def took_owners(sem, ref):
+        @pl.when(owner)
+        def _():
+            took(sem, ref, n_own - 1)
+
+        @pl.when(jnp.logical_not(owner))
+        def _():
+            took(sem, ref, n_own)
 
     def column_peers(phase, src, dst):
         i = PHASES.index(phase)
@@ -214,27 +247,32 @@
             for j in range(n_bn):
                 for r in range(subs):
                     low = j * block + r * LANES
-                    send[:, j, at + r, :] = values[:, low : low + LANES]
-        recv[me] = send[d, b]
-        all_peers(phase, lambda g, j: send.at[g, j], recv)
+                    block_rows = values[:, low : low + LANES]
+                    for g in range(n_dp):
+                        flat = g * n_bn + j
+                        send[flat // 2, flat % 2, at + r, :] = block_rows[g]
+        to_owners(phase, send, recv)
 
     def send_norm(phase_in, phase_out, recv, own, stat):
-        arrived(phase_in, recv)
-        subs = recv.shape[1] // 2
-        both = jnp.sum(recv[...], axis=0)
-        mean = both[:subs] * (1.0 / total)
-        spread = both[subs:]
-        for e in range(n_dp):
-            part = recv[e * n_bn : (e + 1) * n_bn][:, :subs]
-            off = jnp.sum(jnp.square(part - counts[e] * mean[None]), axis=0)
-            spread = spread + off / jnp.maximum(counts[e], 1.0)
-        own[:subs] = mean
-        own[subs:] = lax.rsqrt(spread * (1.0 / total) + EPS_BN)
-        stat[me] = own[...]
-        all_peers(phase_out, lambda g, j: own, stat)
+        @pl.when(owner)
+        def _():
+            took(recv_sem.at[PHASES.index(phase_in)], recv, n_dev - 1)
+            subs = recv.shape[2] // 2
+            both = jnp.sum(recv[...], axis=0)
+            mean = both[:, :subs] * (1.0 / total)
+            spread = both[:, subs:]
+            for e in range(n_dp):
+                part = recv[e * n_bn : (e + 1) * n_bn][:, :, :subs]
+                off = jnp.sum(jnp.square(part - counts[e] * mean[None]), axis=0)
+                spread = spread + off / jnp.maximum(counts[e], 1.0)
+            own[:, :subs] = mean
+            own[:, subs:] = lax.rsqrt(spread * (1.0 / total) + EPS_BN)
+            stat[mine_at] = own[...]
+            for peer in peers:
+                push(phase_out, own, stat.at[mine_at], peer)
 
     def tables(phase, stat, width):
-        arrived(phase, stat)
+        took_owners(recv_sem.at[PHASES.index(phase)], stat)
         block = width // n_bn
         subs = block // LANES
         held = stat[...].reshape(n_dp, n_bn, 2 * subs, LANES)
@@ -275,8 +313,11 @@
         if i == 0:
             for load in loads[4:]:
                 load.start()
+            pl.semaphore_wait(barrier, n_dp + n_bn - 2)
+            for j in bns[1:]:
+                pl.semaphore_signal(ready_sem, inc=1, device_id=(d, j), device_id_type=MESH)
     h_ref[...] = first
-    pl.semaphore_wait(barrier, n_dev - 1)
+    pl.semaphore_wait(ready_sem, n_bn - 1)
     column_peers("query", query_own, query_all)
     send_sums("sum1", h_ref[...], send1, recv1)
     part = jnp.zeros((8, n_dp * slots), f32)
@@ -349,8 +390,14 @@
     logit = jnp.sum(jnp.where(chosen, pairs, 0.0), axis=0, keepdims=True) * INV_TEMP
     loss_ref[...] = jnp.log(jnp.exp(logit - INV_TEMP) + negative) + INV_TEMP - logit
 
-    for phase, dst in zip(PHASES, (query_all, recv1, stat1, recv2, stat2, recv3, stat3, part_all, key_all)):
+    for phase, dst in (("query", query_all), ("queue", part_all), ("key", key_all)):
         sent(phase, dst)
+    for i, send, recv in ((1, send1, recv1), (3, send2, recv2), (5, send3, recv3)):
+        took_owners(send_sem.at[i], send)
+
+        @pl.when(owner)
+        def _():
+            took(send_sem.at[i + 1], recv, n_dev - 1)
 
 
 def on_device_fixed(n_dp, n_bn, features, shuffle_masks, conv_in, conv_mid, conv_out, head, queries, queue, positive):
@@ -364,10 +411,10 @@
     def exchange(c):
         tile = (2 * (c // n_bn // LANES), LANES)
         return [
-            pltpu.VMEM((n_dp, n_bn) + tile, f32),
-            pltpu.VMEM((n_dev,) + tile, f32),
-            pltpu.VMEM(tile, f32),
-            pltpu.VMEM((n_dev,) + tile, f32),
+            pltpu.VMEM((n_dev // 2, 2) + tile, f32),
+            pltpu.VMEM((n_dev, 2) + tile, f32),
+            pltpu.VMEM((2,) + tile, f32),
+            pltpu.VMEM((n_dev // 2, 2) + tile, f32),
         ]
 
     vmem = pl.BlockSpec(memory_space=pltpu.VMEM)
@@ -406,6 +453,7 @@
             pltpu.SemaphoreType.DMA((PANELS,)),
             pltpu.SemaphoreType.DMA((len(PHASES),)),
             pltpu.SemaphoreType.DMA((len(PHASES),)),
+            pltpu.SemaphoreType.REGULAR,
         ],
         compiler_params=pltpu.CompilerParams(
             collective_id=0, has_side_effects=True, vmem_limit_bytes=64 << 20
@@ -418,7 +466,7 @@
 def on_device(n_dp, n_bn, *arrays):
     features, conv_in = arrays[0], arrays[2]
     whole_lanes = conv_in.shape[1] % (n_bn * LANES) == 0 and features.shape[2] % (n_bn * LANES) == 0
-    if whole_lanes and n_dp <= features.shape[0] and features.shape[1] == 8:
+    if whole_lanes and n_bn % 2 == 0 and n_dp * n_bn % 4 == 0 and n_dp <= features.shape[0] and features.shape[1] == 8:
         return on_device_fixed(n_dp, n_bn, *arrays)
     return on_device_moving(*arrays)
 

time: 45.9 us -> 45.8 us (level)
  no operation moved by 1% of the time
where the time goes in v3:
time: 45.8 us; the launch traced here: 45.6 us
  Pallas kernels  44.4 us (97%)
  local copies, waits for them, and re-layouts  1.19 us (3%)
    pallas_call x1, Pallas kernels, on_device_fixed(): pl.pallas_call(functools.partial(fixed_kernel, n_dp, n_bn), out_shape=jax...  44.4 us
    unnamed x1, local copies, waits for them, and re-layouts  1.19 us

profile of v3, /device:TPU:0, one launch (start us, length us, event | category | flops | bytes accessed | tf_op | source)
XLA Modules:
  0.0 45.6 jit_solution(9558472075394528991)
XLA Ops:
  0.0 44.4 %fixed_crops.1 = f32[1,16]{1,0:T(1,128)} custom-call(s32[16]{0:T(128)} %masks_hbm.1, s32[16]{0:T(128)} %positive_hbm.1, bf16[16,128]{1,0:T(8,128)(2,1)} %queries_hbm.1, bf16[128,2048]{1,0:T(8,128)(2,1)} %bitcast.2, bf16[2048,512]{1,0:T(8,128)(2,1)} %in_hbm.1, bf16[3,512,512]{2,1,0:T(8,128)(2,1)} %mid_hbm.1, bf16[512,2048]{1,0:T(8,128)(2,1)} %out_hbm.1, ...), custom_call_target="tpu_custom_call" | custom-call | tf_op jit(solution)/shard_map/fixed_crops/pallas_call | solution.py:422
  44.4 1.2 %copy.11 = f32[16]{0:T(128)} copy(f32[16]{0:T(128)} %bitcast.3) | data formatting | bytes 128

commit v4 on v3

--- a/solution.py
+++ b/solution.py
@@ -104,7 +104,7 @@
     h_ref, wide_ref, mean_ref, scale_ref,
     send1, recv1, own1, stat1, send2, recv2, own2, stat2, send3, recv3, own3, stat3,
     query_own, query_all, part_own, part_all, key_own, key_all,
-    load_sem, panel_sem, send_sem, recv_sem, ready_sem,
+    load_sem, panel_sem, send_sem, recv_sem,
 ):
     f32, bf16 = jnp.float32, jnp.bfloat16
     n_dev = n_dp * n_bn
@@ -137,10 +137,8 @@
 
     dps = [lax.rem(d + k, n_dp) for k in range(n_dp)]
     bns = [lax.rem(b + k, n_bn) for k in range(n_bn)]
-    order = [k for k in (n_dp // 2 + i * o for i in range(n_dp // 2) for o in (1, -1))]
-    order = list(dict.fromkeys(order + list(range(n_dp))))
-    peers = [(dps[k % n_dp], j) for k in order if k % n_dp for j in bns] + [(d, j) for j in bns[1:]]
-    for peer in [(g, b) for g in dps[1:]] + [(d, j) for j in bns[1:]]:
+    peers = [(g, j) for g in dps for j in bns][1:]
+    for peer in peers:
         pl.semaphore_signal(barrier, inc=1, device_id=peer, device_id_type=MESH)
 
     n_own = n_dev // 2
@@ -313,20 +311,17 @@
         if i == 0:
             for load in loads[4:]:
                 load.start()
-            pl.semaphore_wait(barrier, n_dp + n_bn - 2)
-            for j in bns[1:]:
-                pl.semaphore_signal(ready_sem, inc=1, device_id=(d, j), device_id_type=MESH)
     h_ref[...] = first
-    pl.semaphore_wait(ready_sem, n_bn - 1)
+    pl.semaphore_wait(barrier, n_dev - 1)
     column_peers("query", query_own, query_all)
     send_sums("sum1", h_ref[...], send1, recv1)
     part = jnp.zeros((8, n_dp * slots), f32)
     loads[4].wait()
     arrived("query", query_all)
-    part = queue_steps(0, 2, part)
+    part = queue_steps(0, 1, part)
     send_norm("sum1", "norm1", recv1, own1, stat1)
     loads[5].wait()
-    part = queue_steps(2, 3, part)
+    part = queue_steps(1, 3, part)
     tables("norm1", stat1, middle)
 
     for s in range(slots):
@@ -453,7 +448,6 @@
             pltpu.SemaphoreType.DMA((PANELS,)),
             pltpu.SemaphoreType.DMA((len(PHASES),)),
             pltpu.SemaphoreType.DMA((len(PHASES),)),
-            pltpu.SemaphoreType.REGULAR,
         ],
         compiler_params=pltpu.CompilerParams(
             collective_id=0, has_side_effects=True, vmem_limit_bytes=64 << 20

time: 45.8 us -> 45.1 us (0.985)
  Pallas kernels: 44.4 us -> 43.7 us
    pallas_call x1, Pallas kernels: 44.4 us -> 43.7 us  [on_device_fixed(): pl.pallas_call(functools.partial(fixed_kernel, n_dp, n_bn), out_shape=jax...]
where the time goes in v4:
time: 45.1 us; the launch traced here: 44.9 us
  Pallas kernels  43.7 us (97%)
  local copies, waits for them, and re-layouts  1.19 us (3%)
    pallas_call x1, Pallas kernels, on_device_fixed(): pl.pallas_call(functools.partial(fixed_kernel, n_dp, n_bn), out_shape=jax...  43.7 us
    unnamed x1, local copies, waits for them, and re-layouts  1.19 us

profile of v4, /device:TPU:0, one launch (start us, length us, event | category | flops | bytes accessed | tf_op | source)
XLA Modules:
  0.0 44.9 jit_solution(13101825522164195821)
XLA Ops:
  0.0 43.7 %fixed_crops.1 = f32[1,16]{1,0:T(1,128)} custom-call(s32[16]{0:T(128)} %masks_hbm.1, s32[16]{0:T(128)} %positive_hbm.1, bf16[16,128]{1,0:T(8,128)(2,1)} %queries_hbm.1, bf16[128,2048]{1,0:T(8,128)(2,1)} %bitcast.2, bf16[2048,512]{1,0:T(8,128)(2,1)} %in_hbm.1, bf16[3,512,512]{2,1,0:T(8,128)(2,1)} %mid_hbm.1, bf16[512,2048]{1,0:T(8,128)(2,1)} %out_hbm.1, ...), custom_call_target="tpu_custom_call" | custom-call | tf_op jit(solution)/shard_map/fixed_crops/pallas_call | solution.py:417
  43.7 1.2 %copy.11 = f32[16]{0:T(128)} copy(f32[16]{0:T(128)} %bitcast.3) | data formatting | bytes 128
